TPU v7x, 256 devices: a whole 4x4x8 slice. The times are simulated.
256 devices in a mesh: tm: 32 (over y, z), row: 8 (over x, core).
Axes of the slice: x: 4, y: 4, z: 8, core: 2. Of those that a mesh axis runs over, the one named last changes fastest.
Arguments:
- precisions: float32 [32, 1024, 1024], P('tm', 'row'), as said below
- couplings: float32 [32, 1024, 1024], P('tm', 'row'), as said below
- right_sides: float32 [32, 1024, 256], P('tm', 'row'), may hold values from -6 to 6
Outputs:
- pivot_blocks: float32 [32, 1024, 1024], P('tm', 'row')
- coupling_blocks: float32 [32, 1024, 1024], P('tm', 'row')
- reduced_sides: float32 [32, 1024, 256], P('tm', 'row')
Inputs may be any that keep to these rules, and one draw needn't show every extreme that they name: precisions and couplings together form a symmetric positive definite block-tridiagonal matrix whose eigenvalues are 1 or more; couplings[0] is zero. `couplings`: see precisions.
All inputs are finite; a program needn't handle non-finite values.
Results may differ from a plain program's by a relative error of at most 0.00023.
Values sent between devices are 32-bit elements; how exact they have to be, the bound alone decides.
No kernel may reach another device: no remote copies, remote signals or barrier semaphores. Data moves between devices by JAX's collectives and lax.ppermute only.
A program may use at most 128 MiB of HBM per device.

v0:
```python
import jax
import jax.numpy as jnp
from jax import lax
from jax.sharding import PartitionSpec as P

LEVELS = 2


def from_behind(block, axis, distance):
    devices = range(lax.axis_size(axis))
    route = [(i - distance, i) for i in devices if i - distance in devices]
    return lax.ppermute(block, axis, route)


def contract(left, right):
    return lax.dot_general(left, right, (((0,), (0,)), ((), ())), precision=lax.Precision.HIGHEST)


def split_cholesky(matrix):
    order = matrix.shape[0]
    if order <= 512:
        return jnp.linalg.cholesky(matrix)
    half = order // 2
    upper_factor = split_cholesky(matrix[:half, :half])
    solved_cols = jax.scipy.linalg.solve_triangular(upper_factor, matrix[:half, half:], lower=True)
    lower_left = solved_cols.T
    remainder = matrix[half:, half:] - contract(solved_cols, solved_cols)
    lower_factor = split_cholesky(remainder)
    top_rows = jnp.concatenate(
        [upper_factor, jnp.zeros((half, order - half), matrix.dtype)], axis=1
    )
    bottom_rows = jnp.concatenate([lower_left, lower_factor], axis=1)
    return jnp.concatenate([top_rows, bottom_rows], axis=0)


def local(precisions, couplings, right_sides):
    diagonal_pivot_rows = precisions[0]
    offdiag_coupling_rows = couplings[0]
    rhs_side_rows = right_sides[0]
    row_count = diagonal_pivot_rows.shape[0]
    block_position = lax.axis_index("tm")
    row_start = lax.axis_index("row") * row_count
    offdiag_coupling_rows = jnp.where(
        block_position == 0, jnp.zeros_like(offdiag_coupling_rows), offdiag_coupling_rows
    )
    for level_step in range(LEVELS):
        level_stride = 1 << level_step
        whole_pivot, whole_coupling, whole_side = (
            lax.all_gather(diagonal_pivot_rows, "row", axis=0, tiled=True),
            lax.all_gather(offdiag_coupling_rows, "row", axis=0, tiled=True),
            lax.all_gather(rhs_side_rows, "row", axis=0, tiled=True),
        )
        next_coupling = from_behind(whole_coupling, "tm", -level_stride)
        factor = split_cholesky(whole_pivot)
        left_part = jax.scipy.linalg.cho_solve((factor, True), offdiag_coupling_rows.T)
        right_cols = lax.dynamic_slice_in_dim(next_coupling, row_start, row_count, 1)
        right_part = jax.scipy.linalg.cho_solve((factor, True), right_cols)
        left_block = lax.dot_general(
            left_part, whole_coupling, (((0,), (1,)), ((), ())), precision=lax.Precision.HIGHEST
        )
        left_side = contract(left_part, whole_side)
        right_block = contract(right_part, next_coupling)
        right_side = contract(right_part, whole_side)
        new_coupling = -contract(left_part, next_coupling)
        received_following = from_behind((left_block, left_side), "tm", -level_stride)
        received_previous = from_behind((right_block, right_side, new_coupling), "tm", level_stride)
        diagonal_pivot_rows = diagonal_pivot_rows - received_following[0] - received_previous[0]
        rhs_side_rows = rhs_side_rows - received_following[1] - received_previous[1]
        offdiag_coupling_rows = received_previous[2]
    return (diagonal_pivot_rows[None], offdiag_coupling_rows[None], rhs_side_rows[None])


def solution(mesh):
    placed = (P("tm", "row", None), P("tm", "row", None), P("tm", "row", None))
    return jax.shard_map(
        local,
        mesh=mesh,
        in_specs=placed,
        out_specs=(P("tm", "row", None), P("tm", "row", None), P("tm", "row", None)),
        check_vma=False,
    )
```

profile of v0, /device:TPU:8, one launch (start us, length us, event | category | flops | bytes accessed | tf_op | source)
XLA Modules:
  0.0 1219.0 jit_solution(4765637610458641546)
XLA Ops:
  13.9 38.0 %all-gather.16.cloned.1.call-done = f32[1,1024,1024]{1,2,0:T(8,128)} async-done(((f32[1,128,1024]{1,2,0:T(8,128)}), f32[1,1024,1024]{1,2,0:T(8,128)}) %all-gather.16.cloned.1.call-update) | async-done | bytes 4194320 | tf_op jit(solution)/shard_map/all_gather | solution.py:49
  55.0 11.7 cholesky.462
  77.4 11.7 cholesky.481
  99.8 11.7 cholesky.502
  122.6 11.7 cholesky.519
  156.4 39.3 %custom-call.44 = f32[4,128,128]{1,2,0:T(8,128)S(1)} custom-call(f32[4,128,128]{2,1,0:T(8,128)S(1)} %get-tuple-element.46), custom_call_target="InvertDiagBlocksLowerTriangular" | custom-call | tf_op jit(solution)/shard_map/jit(_solve_triangular)/triangular_solve | solution.py:25
  213.0 11.7 cholesky.534
  240.0 13.2 %cholesky.553 = f32[128,128]{1,0:T(8,128)} custom-call(f32[128,128]{1,0:T(8,128)} %cholesky.763), custom_call_target="Cholesky" | custom-call | tf_op jit(solution)/shard_map/jit(cholesky)/cholesky | solution.py:22
  266.8 11.9 cholesky.574
  290.6 11.7 cholesky.591
  308.1 23.2 %while.13 = (s32[]{:T(128)}, f32[1024,1024]{1,0:T(8,128)}, s32[8,2]{0,1:T(2,128)S(1)}, f32[8,128,128]{2,1,0:T(8,128)S(1)}, s32[]{:T(128)}) while((s32[]{:T(128)}, f32[1024,1024]{1,0:T(8,128)}, s32[8,2]{0,1:T(2,128)S(1)}, f32[8,128,128]{2,1,0:T(8,128)S(1)}, s32[]{:T(128)}) %tuple.193), condition=%wide.while_cond.1, body=%wide.while_body.1.sunk | while | flops 2 | bytes 131181 | solution.py:55
  331.3 78.6 %custom-call.48 = f32[8,128,128]{1,2,0:T(8,128)S(1)} custom-call(f32[8,128,128]{2,1,0:T(8,128)S(1)} %get-tuple-element.47), custom_call_target="InvertDiagBlocksLowerTriangular" | custom-call | tf_op jit(solution)/shard_map/jit(_cho_solve)/triangular_solve | solution.py:55
  440.3 66.3 %collective-permute-done.1 = f32[1024,1024]{1,0:T(8,128)S(1)} collective-permute-done((f32[1024,1024]{1,0:T(8,128)}, f32[1024,1024]{1,0:T(8,128)S(1)}, u32[]{:S(2)}, u32[]{:S(2)}) %collective-permute-start.1) | collective-permute-done | bytes 4194336 | tf_op jit(solution)/shard_map/ppermute | solution.py:12
  527.6 14.7 %collective-permute-done.2 = f32[128,1024]{0,1:T(8,128)S(1)} collective-permute-done((f32[128,1024]{0,1:T(8,128)S(1)}, f32[128,1024]{0,1:T(8,128)S(1)}, u32[]{:S(2)}, u32[]{:S(2)}) %collective-permute-start.2) | collective-permute-done | bytes 524320 | tf_op jit(solution)/shard_map/ppermute | solution.py:12
  549.8 14.0 %collective-permute-done.3 = f32[128,1024]{1,0:T(8,128)S(1)} collective-permute-done((f32[128,1024]{1,0:T(8,128)S(1)}, f32[128,1024]{1,0:T(8,128)S(1)}, u32[]{:S(2)}, u32[]{:S(2)}) %collective-permute-start.3) | collective-permute-done | bytes 524320 | tf_op jit(solution)/shard_map/ppermute | solution.py:12
  584.0 11.7 cholesky.606
  606.4 11.7 cholesky.625
  653.2 11.7 cholesky.663
  676.2 39.3 %custom-call.53 = f32[4,128,128]{1,2,0:T(8,128)S(1)} custom-call(f32[4,128,128]{2,1,0:T(8,128)S(1)} %get-tuple-element.49), custom_call_target="InvertDiagBlocksLowerTriangular" | custom-call | tf_op jit(solution)/shard_map/jit(_solve_triangular)/triangular_solve | solution.py:25
  758.8 13.2 %cholesky.697 = f32[128,128]{1,0:T(8,128)} custom-call(f32[128,128]{1,0:T(8,128)} %cholesky.789), custom_call_target="Cholesky" | custom-call | tf_op jit(solution)/shard_map/jit(cholesky)/cholesky | solution.py:22
  785.5 12.1 cholesky.718
  827.1 22.7 %while.15 = (s32[]{:T(128)}, f32[1024,1024]{1,0:T(8,128)}, s32[8,2]{0,1:T(2,128)S(1)}, f32[8,128,128]{2,1,0:T(8,128)S(1)}, s32[]{:T(128)}) while((s32[]{:T(128)}, f32[1024,1024]{1,0:T(8,128)}, s32[8,2]{0,1:T(2,128)S(1)}, f32[8,128,128]{2,1,0:T(8,128)S(1)}, s32[]{:T(128)}) %tuple.216), condition=%wide.while_cond.1.clone.1, body=%wide.while_body.1.clone.1.sunk | while | flops 2 | bytes 131181 | solution.py:55
  849.8 78.8 %custom-call.57 = f32[8,128,128]{1,2,0:T(8,128)S(1)} custom-call(f32[8,128,128]{2,1,0:T(8,128)S(1)} %get-tuple-element.50), custom_call_target="InvertDiagBlocksLowerTriangular" | custom-call | tf_op jit(solution)/shard_map/jit(_cho_solve)/triangular_solve | solution.py:55
  977.8 174.4 %collective-permute-done.5 = f32[1024,1024]{1,0:T(8,128)} collective-permute-done((f32[1024,1024]{1,0:T(8,128)}, f32[1024,1024]{1,0:T(8,128)}, u32[]{:S(2)}, u32[]{:S(2)}) %collective-permute-start.5) | collective-permute-done | bytes 4194336 | tf_op jit(solution)/shard_map/ppermute | solution.py:12
  (520 shorter events, 507.7 us)
Async XLA Ops:
  7.2 44.7 %all-gather.16.cloned.1.call-start = ((), (), s32[]{:S(2)}) async-start(), calls=%async_computation.3 | async-start | bytes 4718592 | tf_op jit(solution)/shard_map/all_gather | solution.py:49
  9.3 400.7 %all-gather.18.cloned.1.call-start = ((), (), s32[]{:S(2)}) async-start(), calls=%async_computation.4 | async-start | bytes 4718592 | tf_op jit(solution)/shard_map/all_gather | solution.py:50
  11.2 553.5 %all-gather.20.cloned.1.call-start = ((), (), s32[]{:S(2)}) async-start(), calls=%async_computation.5 | async-start | bytes 1179648 | tf_op jit(solution)/shard_map/all_gather | solution.py:51
  12.0 568.9 %all-gather.10.cloned.1.call-start = ((), (), s32[]{:S(2)}) async-start(), calls=%async_computation | async-start | bytes 4718592 | tf_op jit(solution)/shard_map/all_gather | solution.py:49
  305.5 110.1 %copy-start.15 = (f32[1024,128]{0,1:T(8,128)S(1)}, f32[1024,128]{0,1:T(8,128)}, u32[]{:S(2)}) copy-start(f32[1024,128]{0,1:T(8,128)} %fusion.497) | copy-start | bytes 1572868
  410.0 96.7 %collective-permute-start.1 = (f32[1024,1024]{1,0:T(8,128)}, f32[1024,1024]{1,0:T(8,128)S(1)}, u32[]{:S(2)}, u32[]{:S(2)}) collective-permute-start(f32[1024,1024]{1,0:T(8,128)} %bitcast.470), channel_id=1, source_target_pairs={{8,0},{16,8},{24,16},{32,24},{40,32},{48,40},{56,48},{64,56},{72,6... | collective-permute-start | bytes 12582920 | tf_op jit(solution)/shard_map/ppermute | solution.py:12
  437.0 90.6 %collective-permute-start = (f32[128,1024]{0,1:T(8,128)S(1)}, f32[128,1024]{0,1:T(8,128)S(1)}, u32[]{:S(2)}, u32[]{:S(2)}) collective-permute-start(f32[128,1024]{0,1:T(8,128)S(1)} %fusion.389), channel_id=1, source_target_pairs={{8,0},{16,8},{24,16},{32,24},{40,32},{48,40},{56,48},{64,56},{72,6... | collective-permute-start | bytes 1572872 | tf_op jit(solution)/shard_map/ppermute | solution.py:12
  525.1 17.3 %collective-permute-start.2 = (f32[128,1024]{0,1:T(8,128)S(1)}, f32[128,1024]{0,1:T(8,128)S(1)}, u32[]{:S(2)}, u32[]{:S(2)}) collective-permute-start(f32[128,1024]{0,1:T(8,128)S(1)} %fusion.395), channel_id=1, source_target_pairs={{0,8},{8,16},{16,24},{24,32},{32,40},{40,48},{48,56},{56,64},{64,7... | collective-permute-start | bytes 1572872 | tf_op jit(solution)/shard_map/ppermute | solution.py:12
  543.2 37.0 %copy-start.17 = (f32[1,128,256]{2,1,0:T(8,128)S(1)}, f32[1,128,256]{2,1,0:T(8,128)}, u32[]{:S(2)}) copy-start(f32[1,128,256]{2,1,0:T(8,128)} %param.10) | copy-start | bytes 393220
  543.2 408.4 %all-gather.12.cloned.1.call-start = ((), (), s32[]{:S(2)}) async-start(), calls=%async_computation.1 | async-start | bytes 4718592 | tf_op jit(solution)/shard_map/all_gather | solution.py:50
  547.9 16.0 %collective-permute-start.3 = (f32[128,1024]{1,0:T(8,128)S(1)}, f32[128,1024]{1,0:T(8,128)S(1)}, u32[]{:S(2)}, u32[]{:S(2)}) collective-permute-start(f32[128,1024]{1,0:T(8,128)S(1)} %convolution_negate_fusion.1), channel_id=1, source_target_pairs={{0,8},{8,16},{16,24},{24,32},{32,40},{40,48},{48,56},{56,64},{64,7... | collective-permute-start | bytes 1572872 | tf_op jit(solution)/shard_map/ppermute | solution.py:12
  564.7 398.9 %all-gather.14.cloned.1.call-start = ((), (), s32[]{:S(2)}) async-start(), calls=%async_computation.2 | async-start | bytes 1179648 | tf_op jit(solution)/shard_map/all_gather | solution.py:51
  567.0 8.3 collective-permute-start.8
  571.2 9.0 collective-permute-start.9
  827.1 111.4 %copy-start.14 = (f32[128,1024]{1,0:T(8,128)S(1)}, f32[128,1024]{1,0:T(8,128)}, u32[]{:S(2)}) copy-start(f32[128,1024]{1,0:T(8,128)} %copy-done.13) | copy-start | bytes 1572868
  951.6 200.6 %collective-permute-start.5 = (f32[1024,1024]{1,0:T(8,128)}, f32[1024,1024]{1,0:T(8,128)}, u32[]{:S(2)}, u32[]{:S(2)}) collective-permute-start(f32[1024,1024]{1,0:T(8,128)} %all-gather.12.cloned.1.call-done), channel_id=1, source_target_pairs={{16,0},{24,8},{32,16},{40,24},{48,32},{56,40},{64,48},{72,56},{80,... | collective-permute-start | bytes 12582920 | tf_op jit(solution)/shard_map/ppermute | solution.py:12
  963.6 189.8 %copy-start = (f32[1024,1024]{1,0:T(8,128)S(1)}, f32[1024,1024]{1,0:T(8,128)}, u32[]{:S(2)}) copy-start(f32[1024,1024]{1,0:T(8,128)} %get-tuple-element.457) | copy-start | bytes 12582916
  966.0 232.4 %collective-permute-start.10 = (f32[128,256]{1,0:T(8,128)S(1)}, f32[128,256]{1,0:T(8,128)S(1)}, u32[]{:S(2)}, u32[]{:S(2)}) collective-permute-start(f32[128,256]{1,0:T(8,128)S(1)} %fusion.398), channel_id=1, source_target_pairs={{16,0},{24,8},{32,16},{40,24},{48,32},{56,40},{64,48},{72,56},{80,... | collective-permute-start | bytes 393224 | tf_op jit(solution)/shard_map/ppermute | solution.py:12
  975.3 234.5 %collective-permute-start.4 = (f32[128,1024]{0,1:T(8,128)S(1)}, f32[128,1024]{0,1:T(8,128)S(1)}, u32[]{:S(2)}, u32[]{:S(2)}) collective-permute-start(f32[128,1024]{0,1:T(8,128)S(1)} %fusion.396), channel_id=1, source_target_pairs={{16,0},{24,8},{32,16},{40,24},{48,32},{56,40},{64,48},{72,56},{80,... | collective-permute-start | bytes 1572872 | tf_op jit(solution)/shard_map/ppermute | solution.py:12
  1175.1 34.0 %copy-start.16 = (f32[128,256]{1,0:T(8,128)S(1)}, f32[128,256]{1,0:T(8,128)}, u32[]{:S(2)}) copy-start(f32[128,256]{1,0:T(8,128)} %fusion.247) | copy-start | bytes 393220
  1175.2 34.7 %copy-start.4 = (f32[128,1024]{0,1:T(8,128)S(1)}, f32[128,1024]{0,1:T(8,128)}, u32[]{:S(2)}) copy-start(f32[128,1024]{0,1:T(8,128)} %fusion.33) | copy-start | bytes 1572868
  1175.2 34.7 %collective-permute-start.7 = (f32[128,1024]{1,0:T(8,128)S(1)}, f32[128,1024]{1,0:T(8,128)S(1)}, u32[]{:S(2)}, u32[]{:S(2)}) collective-permute-start(f32[128,1024]{1,0:T(8,128)S(1)} %convolution_negate_fusion), channel_id=1, source_target_pairs={{0,16},{8,24},{16,32},{24,40},{32,48},{40,56},{48,64},{56,72},{64,... | collective-permute-start | bytes 1572872 | tf_op jit(solution)/shard_map/ppermute | solution.py:12
  1189.1 20.7 %collective-permute-start.6 = (f32[128,1024]{0,1:T(8,128)S(1)}, f32[128,1024]{0,1:T(8,128)S(1)}, u32[]{:S(2)}, u32[]{:S(2)}) collective-permute-start(f32[128,1024]{0,1:T(8,128)S(1)} %fusion.397), channel_id=1, source_target_pairs={{0,16},{8,24},{16,32},{24,40},{32,48},{40,56},{48,64},{56,72},{64,... | collective-permute-start | bytes 1572872 | tf_op jit(solution)/shard_map/ppermute | solution.py:12
  1194.2 15.0 %collective-permute-start.11 = (f32[128,256]{1,0:T(8,128)S(1)}, f32[128,256]{1,0:T(8,128)S(1)}, u32[]{:S(2)}, u32[]{:S(2)}) collective-permute-start(f32[128,256]{1,0:T(8,128)S(1)} %fusion.399), channel_id=1, source_target_pairs={{0,16},{8,24},{16,32},{24,40},{32,48},{40,56},{48,64},{56,72},{64,... | collective-permute-start | bytes 393224 | tf_op jit(solution)/shard_map/ppermute | solution.py:12
  (16 other events, 101.1 us)
Sparse Core Ops, SparseCore 0:
  10.4 41.4 all-gather.15
  53.8 35.9 all-gather.17
  91.6 25.9 all-gather.19
  543.3 37.1 all-gather.9
  582.8 35.7 all-gather.11
  620.9 26.0 all-gather.13
where the time goes:
time: 1230 us; the launch traced here: 1220 us
  other arithmetic  586 us (48%)
  waiting for transfers between devices  324 us (26%)
  matrix products  156 us (13%)
  local copies, waits for them, and re-layouts  79.8 us (6%)
  starting transfers between devices  45.5 us (4%)
  between operations  27.1 us (2%)
    another operation x59, other arithmetic, split_cholesky(): return jnp.linalg.cholesky(matrix)  332 us
    ppermute x12, waiting for transfers between devices, from_behind(): return lax.ppermute(block, axis, route)  285 us
    another operation x5, other arithmetic, local(): jax.scipy.linalg.cho_solve((factor, True), offdiag_coupling_rows.T)  162 us
    another operation x5, other arithmetic, split_cholesky(): jax.scipy.linalg.solve_triangular(upper_factor, matrix[:half, half:], low...  79.2 us
    another operation x59, local copies, waits for them, and re-layouts, local(): jax.scipy.linalg.cho_solve((factor, True), offdiag_coupling_rows.T)  45.7 us
    another operation x60, matrix products, local(): jax.scipy.linalg.cho_solve((factor, True), offdiag_coupling_rows.T)  45.7 us
    ppermute x12, starting transfers between devices, from_behind(): return lax.ppermute(block, axis, route)  45.2 us
    dot_general x10, matrix products, contract(): lax.dot_general(left, right, (((0,), (0,)), ((), ())), precision=lax.Prec...  39.6 us
  transfers between devices with their start and end apart: 18, of which 7 were waited for; matrix products, arithmetic and copies ran while one was open for 67% of the time, Pallas kernels for 0%

commit v1 on v0

--- a/solution.py
+++ b/solution.py
@@ -4,6 +4,27 @@
 from jax.sharding import PartitionSpec as P
 
 LEVELS = 2
+
+
+def raise_digits(vals, dim_at):
+    shard_axis = "row"
+    pieces_in = []
+    amount_of = jax.lax.axis_size(shard_axis)
+    for dd in range(amount_of):
+        pieces_in.append((dd, (dd + 1) % amount_of))
+    heap = []
+    for dd in range(amount_of):
+        heap.append((dd, (dd - 1) % amount_of))
+    r_now, ready = ([vals], [vals])
+    for _ in range(amount_of // 2):
+        x_new = jax.lax.ppermute(r_now[-1], shard_axis, pieces_in)
+        r_now.append(x_new)
+    for _ in range((amount_of - 1) // 2):
+        then = jax.lax.ppermute(ready[-1], axis_name=shard_axis, perm=heap)
+        ready.append(then)
+    w_next = jnp.concatenate([*r_now[::-1], *ready[1:]], axis=dim_at)
+    u_next = jax.lax.axis_index(shard_axis)
+    return jnp.roll(w_next, (u_next - amount_of // 2) * vals.shape[dim_at], axis=dim_at)
 
 
 def from_behind(block, axis, distance):
@@ -46,7 +67,7 @@
     for level_step in range(LEVELS):
         level_stride = 1 << level_step
         whole_pivot, whole_coupling, whole_side = (
-            lax.all_gather(diagonal_pivot_rows, "row", axis=0, tiled=True),
+            raise_digits(diagonal_pivot_rows, 0),
             lax.all_gather(offdiag_coupling_rows, "row", axis=0, tiled=True),
             lax.all_gather(rhs_side_rows, "row", axis=0, tiled=True),
         )

time: 1230 us -> 1290 us (1.049)
  waiting for transfers between devices: 324 us -> 351 us
  starting transfers between devices: 45.5 us -> 63.7 us
    ppermute x0 -> x14, waiting for transfers between devices: none -> 61.3 us  [the longest x8 51.8 us: raise_digits(): x_new = jax.lax.ppermute(r_now[-1], shard_axis, pieces_in)]
    all_gather x2 -> x0, waiting for transfers between devices: 38 us -> none  [local(): lax.all_gather(diagonal_pivot_rows, 'row', axis=0, tiled=True)]
    ppermute x0 -> x14, starting transfers between devices: none -> 19.9 us  [the longest x6 14.8 us: raise_digits(): then = jax.lax.ppermute(ready[-1], axis_name=shard_axis, perm=heap)]
    another operation x59, other arithmetic: 332 us -> 318 us  [split_cholesky(): return jnp.linalg.cholesky(matrix)]
  transfers between devices with their start and end apart: 18 -> 30, of which waited for: 7 -> 15; matrix products, arithmetic and copies ran while one was open for 67% -> 65% of each run, Pallas kernels for 0% -> 0%
where the time goes in v1:
time: 1290 us; the launch traced here: 1280 us
  other arithmetic  581 us (45%)
  waiting for transfers between devices  351 us (27%)
  matrix products  168 us (13%)
  local copies, waits for them, and re-layouts  89.6 us (7%)
  starting transfers between devices  63.7 us (5%)
  between operations  26.9 us (2%)
    another operation x59, other arithmetic, split_cholesky(): return jnp.linalg.cholesky(matrix)  318 us
    ppermute x12, waiting for transfers between devices, from_behind(): return lax.ppermute(block, axis, route)  289 us
    another operation x5, other arithmetic, local(): jax.scipy.linalg.cho_solve((factor, True), offdiag_coupling_rows.T)  165 us
    another operation x5, other arithmetic, split_cholesky(): jax.scipy.linalg.solve_triangular(upper_factor, matrix[:half, half:], low...  81.3 us
    ppermute x8, waiting for transfers between devices, raise_digits(): x_new = jax.lax.ppermute(r_now[-1], shard_axis, pieces_in)  51.8 us
    another operation x60, matrix products, local(): jax.scipy.linalg.cho_solve((factor, True), offdiag_coupling_rows.T)  49.9 us
    another operation x59, local copies, waits for them, and re-layouts, local(): jax.scipy.linalg.cho_solve((factor, True), offdiag_coupling_rows.T)  46.6 us
    ppermute x12, starting transfers between devices, from_behind(): return lax.ppermute(block, axis, route)  43.4 us
  transfers between devices with their start and end apart: 30, of which 15 were waited for; matrix products, arithmetic and copies ran while one was open for 65% of the time, Pallas kernels for 0%

profile of v1, /device:TPU:8, one launch (start us, length us, event | category | flops | bytes accessed | tf_op | source)
XLA Modules:
  0.0 1280.4 jit_solution(72083442117897560)
XLA Ops:
  39.8 12.3 collective-permute-done.2
  68.9 11.7 cholesky.462
  91.2 12.1 cholesky.481
  113.9 11.7 cholesky.502
  136.7 11.9 cholesky.519
  153.9 11.9 while.12
  165.7 39.3 %custom-call.44 = f32[4,128,128]{1,2,0:T(8,128)S(1)} custom-call(f32[4,128,128]{2,1,0:T(8,128)S(1)} %get-tuple-element.47), custom_call_target="InvertDiagBlocksLowerTriangular" | custom-call | tf_op jit(solution)/shard_map/jit(_solve_triangular)/triangular_solve | solution.py:46
  224.8 11.7 cholesky.534
  249.8 11.7 cholesky.553
  274.3 11.9 cholesky.574
  298.2 11.7 cholesky.591
  317.0 23.4 %while.13 = (s32[]{:T(128)}, f32[1024,1024]{1,0:T(8,128)}, s32[8,2]{0,1:T(2,128)S(1)}, f32[8,128,128]{2,1,0:T(8,128)S(1)}, s32[]{:T(128)}) while((s32[]{:T(128)}, f32[1024,1024]{1,0:T(8,128)}, s32[8,2]{0,1:T(2,128)S(1)}, f32[8,128,128]{2,1,0:T(8,128)S(1)}, s32[]{:T(128)}) %tuple.194), condition=%wide.while_cond.1, body=%wide.while_body.1.sunk | while | flops 2 | bytes 131181 | solution.py:76
  340.4 78.8 %custom-call.48 = f32[8,128,128]{1,2,0:T(8,128)S(1)} custom-call(f32[8,128,128]{2,1,0:T(8,128)S(1)} %get-tuple-element.48), custom_call_target="InvertDiagBlocksLowerTriangular" | custom-call | tf_op jit(solution)/shard_map/jit(_cho_solve)/triangular_solve | solution.py:76
  461.0 77.4 %collective-permute-done.8 = f32[1024,1024]{1,0:T(8,128)S(1)} collective-permute-done((f32[1024,1024]{1,0:T(8,128)}, f32[1024,1024]{1,0:T(8,128)S(1)}, u32[]{:S(2)}, u32[]{:S(2)}) %collective-permute-start.8) | collective-permute-done | bytes 4194336 | tf_op jit(solution)/shard_map/ppermute | solution.py:33
  646.2 11.7 cholesky.606
  668.6 12.1 cholesky.625
  692.5 11.7 cholesky.646
  715.4 11.9 cholesky.663
  743.4 39.3 %custom-call.53 = f32[4,128,128]{1,2,0:T(8,128)S(1)} custom-call(f32[4,128,128]{2,1,0:T(8,128)S(1)} %get-tuple-element.50), custom_call_target="InvertDiagBlocksLowerTriangular" | custom-call | tf_op jit(solution)/shard_map/jit(_solve_triangular)/triangular_solve | solution.py:46
  802.4 11.7 cholesky.678
  851.9 11.9 cholesky.718
  894.7 23.4 %while.15 = (s32[]{:T(128)}, f32[1024,1024]{1,0:T(8,128)}, s32[8,2]{0,1:T(2,128)S(1)}, f32[8,128,128]{2,1,0:T(8,128)S(1)}, s32[]{:T(128)}) while((s32[]{:T(128)}, f32[1024,1024]{1,0:T(8,128)}, s32[8,2]{0,1:T(2,128)S(1)}, f32[8,128,128]{2,1,0:T(8,128)S(1)}, s32[]{:T(128)}) %tuple.213), condition=%wide.while_cond.1.clone.1, body=%wide.while_body.1.clone.1.sunk | while | flops 2 | bytes 131181 | solution.py:76
  918.2 78.8 %custom-call.57 = f32[8,128,128]{1,2,0:T(8,128)S(1)} custom-call(f32[8,128,128]{2,1,0:T(8,128)S(1)} %get-tuple-element.51), custom_call_target="InvertDiagBlocksLowerTriangular" | custom-call | tf_op jit(solution)/shard_map/jit(_cho_solve)/triangular_solve | solution.py:76
  1040.4 174.9 %collective-permute-done.19 = f32[1024,1024]{1,0:T(8,128)} collective-permute-done((f32[1024,1024]{1,0:T(8,128)}, f32[1024,1024]{1,0:T(8,128)}, u32[]{:S(2)}, u32[]{:S(2)}) %collective-permute-start.19) | collective-permute-done | bytes 4194336 | tf_op jit(solution)/shard_map/ppermute | solution.py:33
  (548 shorter events, 598.3 us)
Async XLA Ops:
  7.2 431.6 %all-gather.11.cloned.1.call-start = ((), (), s32[]{:S(2)}) async-start(), calls=%async_computation.2 | async-start | bytes 4718592 | tf_op jit(solution)/shard_map/all_gather | solution.py:71
  9.1 600.9 %all-gather.13.cloned.1.call-start = ((), (), s32[]{:S(2)}) async-start(), calls=%async_computation.3 | async-start | bytes 1179648 | tf_op jit(solution)/shard_map/all_gather | solution.py:72
  20.2 10.9 collective-permute-start.1
  20.3 16.1 %collective-permute-start.4 = (f32[128,1024]{0,1:T(8,128)S(1)}, f32[128,1024]{0,1:T(8,128)S(1)}, u32[]{:S(2)}, u32[]{:S(2)}) collective-permute-start(f32[128,1024]{0,1:T(8,128)S(1)} %bitcast.466), channel_id=1, source_target_pairs={{0,7},{1,0},{2,1},{3,2},{4,3},{5,4},{6,5},{7,6},{8,15},{9,8},{10,9... | collective-permute-start | bytes 1572872 | tf_op jit(solution)/shard_map/ppermute | solution.py:23
  31.1 21.0 %collective-permute-start.2 = (f32[128,1024]{0,1:T(8,128)S(1)}, f32[128,1024]{0,1:T(8,128)S(1)}, u32[]{:S(2)}, u32[]{:S(2)}) collective-permute-start(f32[128,1024]{0,1:T(8,128)S(1)} %collective-permute-done.1), channel_id=1, source_target_pairs={{0,1},{1,2},{2,3},{3,4},{4,5},{5,6},{6,7},{7,0},{8,9},{9,10},{10,1... | collective-permute-start | bytes 1572872 | tf_op jit(solution)/shard_map/ppermute | solution.py:20
  36.3 17.8 %collective-permute-start.5 = (f32[128,1024]{0,1:T(8,128)S(1)}, f32[128,1024]{0,1:T(8,128)S(1)}, u32[]{:S(2)}, u32[]{:S(2)}) collective-permute-start(f32[128,1024]{0,1:T(8,128)S(1)} %collective-permute-done.4), channel_id=1, source_target_pairs={{0,7},{1,0},{2,1},{3,2},{4,3},{5,4},{6,5},{7,6},{8,15},{9,8},{10,9... | collective-permute-start | bytes 1572872 | tf_op jit(solution)/shard_map/ppermute | solution.py:23
  52.2 964.5 %all-gather.7.cloned.1.call-start = ((), (), s32[]{:S(2)}) async-start(), calls=%async_computation | async-start | bytes 4718592 | tf_op jit(solution)/shard_map/all_gather | solution.py:71
  438.8 99.6 %collective-permute-start.8 = (f32[1024,1024]{1,0:T(8,128)}, f32[1024,1024]{1,0:T(8,128)S(1)}, u32[]{:S(2)}, u32[]{:S(2)}) collective-permute-start(f32[1024,1024]{1,0:T(8,128)} %bitcast.467), channel_id=1, source_target_pairs={{8,0},{16,8},{24,16},{32,24},{40,32},{48,40},{56,48},{64,56},{72,6... | collective-permute-start | bytes 12582920 | tf_op jit(solution)/shard_map/ppermute | solution.py:33
  458.1 117.7 %collective-permute-start.7 = (f32[128,1024]{0,1:T(8,128)S(1)}, f32[128,1024]{0,1:T(8,128)}, u32[]{:S(2)}, u32[]{:S(2)}) collective-permute-start(f32[128,1024]{0,1:T(8,128)S(1)} %fusion.394), channel_id=1, source_target_pairs={{8,0},{16,8},{24,16},{32,24},{40,32},{48,40},{56,48},{64,56},{72,6... | collective-permute-start | bytes 1572872 | tf_op jit(solution)/shard_map/ppermute | solution.py:33
  545.7 13.5 %collective-permute-start.17 = (f32[128,1024]{1,0:T(8,128)S(1)}, f32[128,1024]{1,0:T(8,128)S(1)}, u32[]{:S(2)}, u32[]{:S(2)}) collective-permute-start(f32[128,1024]{1,0:T(8,128)S(1)} %convolution_negate_fusion.1), channel_id=1, source_target_pairs={{0,8},{8,16},{16,24},{24,32},{32,40},{40,48},{48,56},{56,64},{64,7... | collective-permute-start | bytes 1572872 | tf_op jit(solution)/shard_map/ppermute | solution.py:33
  560.1 465.1 %all-gather.9.cloned.1.call-start = ((), (), s32[]{:S(2)}) async-start(), calls=%async_computation.1 | async-start | bytes 1179648 | tf_op jit(solution)/shard_map/all_gather | solution.py:72
  573.9 13.2 %collective-permute-start.9 = (f32[128,1024]{0,1:T(8,128)S(1)}, f32[128,1024]{0,1:T(8,128)S(1)}, u32[]{:S(2)}, u32[]{:S(2)}) collective-permute-start(f32[128,1024]{0,1:T(8,128)S(1)} %fusion.400), channel_id=1, source_target_pairs={{0,8},{8,16},{16,24},{24,32},{32,40},{40,48},{48,56},{56,64},{64,7... | collective-permute-start | bytes 1572872 | tf_op jit(solution)/shard_map/ppermute | solution.py:33
  588.2 10.2 collective-permute-start.10
  601.5 14.8 %collective-permute-start.14 = (f32[128,1024]{0,1:T(8,128)S(1)}, f32[128,1024]{0,1:T(8,128)S(1)}, u32[]{:S(2)}, u32[]{:S(2)}) collective-permute-start(f32[128,1024]{0,1:T(8,128)S(1)} %subtract_subtract_fusion), channel_id=1, source_target_pairs={{0,7},{1,0},{2,1},{3,2},{4,3},{5,4},{6,5},{7,6},{8,15},{9,8},{10,9... | collective-permute-start | bytes 1572872 | tf_op jit(solution)/shard_map/ppermute | solution.py:23
  608.1 10.8 collective-permute-start.12
  613.0 11.7 collective-permute-start.22
  616.3 15.5 %collective-permute-start.15 = (f32[128,1024]{0,1:T(8,128)S(1)}, f32[128,1024]{0,1:T(8,128)S(1)}, u32[]{:S(2)}, u32[]{:S(2)}) collective-permute-start(f32[128,1024]{0,1:T(8,128)S(1)} %collective-permute-done.14), channel_id=1, source_target_pairs={{0,7},{1,0},{2,1},{3,2},{4,3},{5,4},{6,5},{7,6},{8,15},{9,8},{10,9... | collective-permute-start | bytes 1572872 | tf_op jit(solution)/shard_map/ppermute | solution.py:23
  619.0 15.5 %collective-permute-start.13 = (f32[128,1024]{0,1:T(8,128)}, f32[128,1024]{0,1:T(8,128)}, u32[]{:S(2)}, u32[]{:S(2)}) collective-permute-start(f32[128,1024]{0,1:T(8,128)} %collective-permute-done.12), channel_id=1, source_target_pairs={{0,1},{1,2},{2,3},{3,4},{4,5},{5,6},{6,7},{7,0},{8,9},{9,10},{10,1... | collective-permute-start | bytes 1572872 | tf_op jit(solution)/shard_map/ppermute | solution.py:20
  1016.7 198.7 %collective-permute-start.19 = (f32[1024,1024]{1,0:T(8,128)}, f32[1024,1024]{1,0:T(8,128)}, u32[]{:S(2)}, u32[]{:S(2)}) collective-permute-start(f32[1024,1024]{1,0:T(8,128)} %all-gather.7.cloned.1.call-done), channel_id=1, source_target_pairs={{16,0},{24,8},{32,16},{40,24},{48,32},{56,40},{64,48},{72,56},{80,... | collective-permute-start | bytes 12582920 | tf_op jit(solution)/shard_map/ppermute | solution.py:33
  1027.6 232.9 %collective-permute-start.24 = (f32[128,256]{1,0:T(8,128)S(1)}, f32[128,256]{1,0:T(8,128)S(1)}, u32[]{:S(2)}, u32[]{:S(2)}) collective-permute-start(f32[128,256]{1,0:T(8,128)S(1)} %fusion.403), channel_id=1, source_target_pairs={{16,0},{24,8},{32,16},{40,24},{48,32},{56,40},{64,48},{72,56},{80,... | collective-permute-start | bytes 393224 | tf_op jit(solution)/shard_map/ppermute | solution.py:33
  1038.1 233.7 %collective-permute-start.18 = (f32[128,1024]{0,1:T(8,128)S(1)}, f32[128,1024]{0,1:T(8,128)S(1)}, u32[]{:S(2)}, u32[]{:S(2)}) collective-permute-start(f32[128,1024]{0,1:T(8,128)S(1)} %fusion.401), channel_id=1, source_target_pairs={{16,0},{24,8},{32,16},{40,24},{48,32},{56,40},{64,48},{72,56},{80,... | collective-permute-start | bytes 1572872 | tf_op jit(solution)/shard_map/ppermute | solution.py:33
  1238.2 33.6 %collective-permute-start.21 = (f32[128,1024]{1,0:T(8,128)S(1)}, f32[128,1024]{1,0:T(8,128)S(1)}, u32[]{:S(2)}, u32[]{:S(2)}) collective-permute-start(f32[128,1024]{1,0:T(8,128)S(1)} %convolution_negate_fusion), channel_id=1, source_target_pairs={{0,16},{8,24},{16,32},{24,40},{32,48},{40,56},{48,64},{56,72},{64,... | collective-permute-start | bytes 1572872 | tf_op jit(solution)/shard_map/ppermute | solution.py:33
  1249.6 22.2 %collective-permute-start.20 = (f32[128,1024]{0,1:T(8,128)S(1)}, f32[128,1024]{0,1:T(8,128)S(1)}, u32[]{:S(2)}, u32[]{:S(2)}) collective-permute-start(f32[128,1024]{0,1:T(8,128)S(1)} %fusion.402), channel_id=1, source_target_pairs={{0,16},{8,24},{16,32},{24,40},{32,48},{40,56},{48,64},{56,72},{64,... | collective-permute-start | bytes 1572872 | tf_op jit(solution)/shard_map/ppermute | solution.py:33
  1255.2 15.9 %collective-permute-start.25 = (f32[128,256]{1,0:T(8,128)S(1)}, f32[128,256]{1,0:T(8,128)S(1)}, u32[]{:S(2)}, u32[]{:S(2)}) collective-permute-start(f32[128,256]{1,0:T(8,128)S(1)} %fusion.404), channel_id=1, source_target_pairs={{0,16},{8,24},{16,32},{24,40},{32,48},{40,56},{48,64},{56,72},{64,... | collective-permute-start | bytes 393224 | tf_op jit(solution)/shard_map/ppermute | solution.py:33
  (22 other events, 629.1 us)
Sparse Core Ops, SparseCore 0:
  10.4 43.7 all-gather.10
  56.1 26.9 all-gather.12
  560.2 34.4 all-gather.6
  631.9 24.3 all-gather.8
